TPU v7x, 32 devices: a whole 2x2x4 slice. The times are simulated.
32 devices in a mesh: grp: 2 (over x), seq: 8 (over z, y), pool: 2 (over core).
Axes of the slice: x: 2, y: 2, z: 4, core: 2. Of those that a mesh axis runs over, the one named last changes fastest.
Arguments:
- factors: bfloat16 [2, 65536, 160], P('grp', 'seq'), parts along dimension 0, may hold values from -6 to 6
- basis: bfloat16 [2, 160, 1024], P('grp', None, 'pool'), parts along dimension 0, may hold values from -1 to 1
- value_pool: bfloat16 [2, 65536, 1024], P('grp', ('seq', 'pool')), parts along dimension 0, may hold values from -6 to 6
- page_summary: bfloat16 [2, 8192, 1024], P('grp', 'seq', 'pool'), parts along dimension 0, may hold values from -6 to 6
- recent_keys: bfloat16 [2, 64, 1024], P('grp', None, 'pool'), parts along dimension 0, may hold values from -20 to 20
- recent_values: bfloat16 [2, 64, 1024], P('grp', None, 'pool'), parts along dimension 0, may hold values from -6 to 6
- query: bfloat16 [2, 8192], P('grp', 'pool'), parts along dimension 0, may hold values from -8192 to 8192
- selected: int32 [2, 8, 1024], P('grp'), parts along dimension 0, may hold values from 0 to 8191, as said below
- owner_map: int32 [2, 8192], P('grp', 'seq'), parts along dimension 0, may hold values from 0 to 1, as said below
- lengths: int32 [2], P('grp'), parts along dimension 0, may hold values from 32768 to 65536, as said below
Outputs:
- attn: bfloat16 [2, 8192], P('grp', 'pool'), parts along dimension 0
There are 2 independent parts, one for each index of `grp`. A program takes and returns all parts, laid end to end along the dimension named above; each array names one. Nothing has to cross between parts.
Inputs may be any that keep to these rules, and one draw needn't show every extreme that they name: `selected`: for every request and key-value head, 1024 distinct page ids in ascending order, each below ceil(lengths / 8); every aligned block of 1024 pages holds at most 256 of them, and for every request and head some block holds exactly 256. `owner_map`: in every aligned block of 1024 pages of a request exactly half of the pages have owner 1. `lengths`: some request has exactly 65536 tokens.
All inputs are finite; a program needn't handle non-finite values.
Results may differ from a plain program's by a relative error of at most 0.0075.
The roundings to bfloat16 on the way count: a program that leaves them out, or rounds other values in their place, can miss the bound.
Values may be sent and summed in bfloat16 or wider, within the bound.
A program may use at most 128 MiB of HBM per device.

v0:
```python
import math
import jax
import jax.numpy as jnp
import numpy as np
from jax import lax
from jax.sharding import PartitionSpec as P

HD = 128
PAGE = 8
SEL = 1024
CAPMIN = 64
WIN = 64


def partner(x, axis, apart):
    return lax.ppermute(x, axis, [(i, i ^ 1 << apart) for i in range(lax.axis_size(axis))])


def llama_rates(head_dim):
    half_dim = head_dim // 2
    base_rates = 500000.0 ** (-(np.arange(half_dim) * 2.0) / head_dim)
    wavelen = 2.0 * math.pi / base_rates
    smooth = (8192.0 / wavelen - 1.0) / 3.0
    blended = (1.0 - smooth) * base_rates / 8.0 + smooth * base_rates
    return np.where(
        wavelen < 2048.0, base_rates, np.where(wavelen > 8192.0, base_rates / 8.0, blended)
    )


def angle_tables(length, head_dim):
    inv_rates = llama_rates(head_dim)
    coarse = (np.arange(length // 256) * 256.0)[:, None] * inv_rates[None, :]
    fine_angles = (np.arange(256) * 1.0)[:, None] * inv_rates[None, :]
    return (np.cos(coarse), np.sin(coarse), np.cos(fine_angles), np.sin(fine_angles))


def combine_angles(coarse_cos, coarse_sin, fine_cos, fine_sin):
    cosine = (
        coarse_cos[:, None, :] * fine_cos[None, :, :]
        - coarse_sin[:, None, :] * fine_sin[None, :, :]
    )
    sine_table = (
        coarse_sin[:, None, :] * fine_cos[None, :, :]
        + coarse_cos[:, None, :] * fine_sin[None, :, :]
    )
    row_count = coarse_cos.shape[0] * 256
    return (cosine.reshape(row_count, -1), sine_table.reshape(row_count, -1))


def rotate(values, cosine, sine_table):
    half_dim = values.shape[-1] // 2
    first_half = values[..., :half_dim]
    second_half = values[..., half_dim:]
    return jnp.concatenate(
        [
            first_half * cosine - second_half * sine_table,
            second_half * cosine + first_half * sine_table,
        ],
        axis=-1,
    )


def slot_pages(chosen_ids, first_page, pages_dev, capacity):
    before = jnp.sum((chosen_ids < first_page).astype(jnp.int32), axis=-1)
    inside = jnp.sum(
        ((chosen_ids >= first_page) & (chosen_ids < first_page + pages_dev)).astype(jnp.int32),
        axis=-1,
    )
    filler = jnp.zeros(chosen_ids.shape[:-1] + (capacity,), jnp.int32) + first_page
    padded = jnp.concatenate([chosen_ids, filler], axis=-1)
    offsets = before[..., None] + jnp.arange(capacity, dtype=jnp.int32)
    picked = jnp.take_along_axis(padded, offsets, axis=-1)
    slot_live = jnp.arange(capacity, dtype=jnp.int32) < inside[..., None]
    return (jnp.where(slot_live, picked - first_page, 0), slot_live)


def merge_parts(earlier, following):
    peak_a, sum_a, out_a = earlier
    peak_b, sum_b, out_b = following
    joint_peak = jnp.maximum(peak_a, peak_b)
    factor_a = jnp.exp(peak_a - joint_peak)
    factor_b = jnp.exp(peak_b - joint_peak)
    return (
        joint_peak,
        sum_a * factor_a + sum_b * factor_b,
        out_a * factor_a[..., None] + out_b * factor_b[..., None],
    )


def local(
    factors,
    basis,
    value_pool,
    page_summary,
    recent_keys,
    recent_values,
    query,
    selected,
    owner_map,
    lengths,
):
    requests, span_rows, rank_dim = factors.shape
    seq_count = lax.axis_size("seq")
    seq_pos = lax.axis_index("seq")
    core_index = lax.axis_index("pool")
    heads_here = basis.shape[2] // HD
    group_size = query.shape[1] // (heads_here * HD)
    pages_dev = span_rows // PAGE
    half_pages = pages_dev // 2
    capacity = max(CAPMIN, 2 * SEL // seq_count)
    score_scale = HD ** (-0.5)
    first_token = seq_pos * span_rows
    first_page = seq_pos * pages_dev
    tables = angle_tables(span_rows * seq_count, HD)
    blocks = span_rows // 256
    coarse_cos = lax.dynamic_slice_in_dim(
        jnp.asarray(tables[0], jnp.float32), seq_pos * blocks, blocks, 0
    )
    coarse_sin = lax.dynamic_slice_in_dim(
        jnp.asarray(tables[1], jnp.float32), seq_pos * blocks, blocks, 0
    )
    cosine, sine_table = combine_angles(
        coarse_cos,
        coarse_sin,
        jnp.asarray(tables[2], jnp.float32),
        jnp.asarray(tables[3], jnp.float32),
    )
    stacked = jnp.einsum("rtk,rkc->rtc", factors, basis, preferred_element_type=jnp.float32)
    stacked = stacked.reshape(requests, span_rows, heads_here, HD)
    keys_bf = rotate(stacked, cosine[None, :, None, :], sine_table[None, :, None, :]).astype(
        jnp.bfloat16
    )
    positions = first_token + jnp.arange(span_rows, dtype=jnp.int32)
    in_range = positions[None, :] < lengths[:, None]
    page_valid = in_range.reshape(requests, pages_dev, PAGE)
    any_valid = jnp.any(page_valid, axis=2)
    paged_keys = keys_bf.reshape(requests, pages_dev, PAGE, heads_here, HD)
    token_mask = page_valid[:, :, :, None, None]
    low_keys = jnp.min(jnp.where(token_mask, paged_keys, jnp.inf), axis=2)
    high_keys = jnp.max(jnp.where(token_mask, paged_keys, -jnp.inf), axis=2)
    center = jnp.where(
        any_valid[:, :, None, None],
        (low_keys.astype(jnp.float32) + high_keys.astype(jnp.float32)) * 0.5,
        0.0,
    ).astype(jnp.bfloat16)
    queries = query.reshape(requests, heads_here, group_size, HD)
    request_idx = jnp.arange(requests, dtype=jnp.int32)[:, None, None]
    local_heads = jnp.arange(heads_here, dtype=jnp.int32)
    my_heads = (core_index * heads_here + local_heads)[None, :, None]
    other_heads = ((1 - core_index) * heads_here + local_heads)[None, :, None]
    ones_count = jnp.cumsum(owner_map, axis=1)
    zeros_count = jnp.cumsum(1 - owner_map, axis=1)
    page_rank = jnp.where(owner_map == 1, ones_count, zeros_count) - 1
    my_ids = lax.dynamic_slice_in_dim(selected, core_index * heads_here, heads_here, 1)
    other_ids = lax.dynamic_slice_in_dim(selected, (1 - core_index) * heads_here, heads_here, 1)
    my_local, my_live = slot_pages(my_ids, first_page, pages_dev, capacity)
    other_local, other_live = slot_pages(other_ids, first_page, pages_dev, capacity)
    my_owner = owner_map[request_idx, my_local]
    my_rank = page_rank[request_idx, my_local]
    other_owner = owner_map[request_idx, other_local]
    other_rank = page_rank[request_idx, other_local]
    held_here = my_owner == core_index
    other_held = (other_owner == core_index) & other_live
    key_rows = paged_keys[request_idx, my_local, :, local_heads[None, :, None], :]
    exact_scores = (
        jnp.einsum("rhgd,rhcpd->rhgcp", queries, key_rows, preferred_element_type=jnp.float32)
        * score_scale
    )
    token_pos = first_token + my_local[..., None] * PAGE + jnp.arange(PAGE, dtype=jnp.int32)
    exact_ok = my_live[..., None] & (token_pos < lengths[:, None, None, None])
    exact_scores = jnp.where(exact_ok[:, :, None], exact_scores, -jnp.inf)
    chosen_mask = jnp.any(
        (my_local[..., None] == jnp.arange(pages_dev, dtype=jnp.int32)) & my_live[..., None], axis=2
    )
    land_scores = (
        jnp.einsum("rhgd,rphd->rhgp", queries, center, preferred_element_type=jnp.float32)
        * score_scale
    )
    land_ok = any_valid[:, None, :] & jnp.logical_not(chosen_mask)
    land_scores = jnp.where(land_ok[:, :, None, :], land_scores, -jnp.inf)
    row_peak = jnp.maximum(
        jnp.maximum(jnp.max(exact_scores, axis=(3, 4)), jnp.max(land_scores, axis=3)), -1e30
    )
    exact_w = jnp.exp(exact_scores - row_peak[..., None, None])
    land_w = jnp.exp(land_scores - row_peak[..., None])
    weight_sum = jnp.sum(exact_w, axis=(3, 4)) + jnp.sum(land_w, axis=3)
    exact_b = exact_w.astype(jnp.bfloat16)
    land_b = land_w.astype(jnp.bfloat16)
    summary = page_summary.reshape(requests, pages_dev, heads_here, HD)
    partial_value = jnp.einsum(
        "rhgp,rphd->rhgd", land_b, summary, preferred_element_type=jnp.float32
    )
    value_store = value_pool.reshape(requests, half_pages, PAGE, value_pool.shape[2] // HD, HD)
    local_rows = value_store[request_idx, my_rank, :, my_heads, :]
    outgoing_rows = value_store[request_idx, other_rank, :, other_heads, :]
    outgoing = jnp.where(other_held[..., None, None], outgoing_rows, jnp.zeros_like(outgoing_rows))
    incoming = partner(outgoing, "pool", 0)
    value_rows = jnp.where(held_here[..., None, None], local_rows, incoming)
    partial_value = partial_value + jnp.einsum(
        "rhgcp,rhcpd->rhgd", exact_b, value_rows, preferred_element_type=jnp.float32
    )
    recent_k = recent_keys.reshape(requests, WIN, heads_here, HD)
    recent_v = recent_values.reshape(requests, WIN, heads_here, HD)
    recent_scores = (
        jnp.einsum("rhgd,rwhd->rhgw", queries, recent_k, preferred_element_type=jnp.float32)
        * score_scale
    )
    recent_peak = jnp.max(recent_scores, axis=3)
    recent_w = jnp.exp(recent_scores - recent_peak[..., None])
    recent_sum = jnp.sum(recent_w, axis=3)
    recent_out = jnp.einsum(
        "rhgw,rwhd->rhgd",
        recent_w.astype(jnp.bfloat16),
        recent_v,
        preferred_element_type=jnp.float32,
    )
    row_total = requests * heads_here * group_size
    row_share = row_total // seq_count
    got_peak, got_sum, got_out = (
        lax.all_to_all(
            row_peak.reshape(1, row_total), "seq", split_axis=1, concat_axis=0, tiled=True
        ),
        lax.all_to_all(
            weight_sum.reshape(1, row_total), "seq", split_axis=1, concat_axis=0, tiled=True
        ),
        lax.all_to_all(
            partial_value.reshape(1, row_total, HD), "seq", split_axis=1, concat_axis=0, tiled=True
        ),
    )
    joint_peak = jnp.max(got_peak, axis=0)
    factor = jnp.exp(got_peak - joint_peak[None, :])
    summed = jnp.sum(got_sum * factor, axis=0)
    gathered_out = jnp.sum(got_out * factor[..., None], axis=0)
    row_start = seq_pos * row_share
    mine_peak = lax.dynamic_slice_in_dim(recent_peak.reshape(row_total), row_start, row_share, 0)
    mine_sum = lax.dynamic_slice_in_dim(recent_sum.reshape(row_total), row_start, row_share, 0)
    mine_out = lax.dynamic_slice_in_dim(recent_out.reshape(row_total, HD), row_start, row_share, 0)
    final_peak, final_sum, final_out = merge_parts(
        (joint_peak, summed, gathered_out), (mine_peak, mine_sum, mine_out)
    )
    rows_out = (final_out / final_sum[:, None]).astype(jnp.bfloat16)
    all_rows = lax.all_gather(rows_out, "seq", axis=0, tiled=True)
    return all_rows.reshape(requests, heads_here * group_size * HD)


def solution(mesh):
    placed = (
        P("grp", "seq", None),
        P("grp", None, "pool"),
        P("grp", ("seq", "pool"), None),
        P("grp", "seq", "pool"),
        P("grp", None, "pool"),
        P("grp", None, "pool"),
        P("grp", "pool"),
        P("grp", None, None),
        P("grp", "seq"),
        P("grp"),
    )
    return jax.shard_map(
        local, mesh=mesh, in_specs=placed, out_specs=P("grp", "pool"), check_vma=False
    )
```

profile of v0, /device:TPU:0, one launch (start us, length us, event | category | flops | bytes accessed | tf_op | source)
XLA Modules:
  0.0 208.9 jit_solution(5469197252403658698)
XLA Ops:
  0.0 1.1 convert_reduce_fusion.1
  1.1 0.1 fusion.74
  1.2 9.1 %gather_fusion.7 = s32[1024]{0:T(1024)S(1)} fusion(s32[4,1280]{1,0:T(4,128)S(1)} %get-tuple-element.43, s32[1024]{0:T(1024)S(1)} %bitcast.168), kind=kCustom, calls=%fused_computation.clone | custom fusion | bytes 16384 | tf_op jit(solution)/shard_map/jit(take_along_axis)/gather | solution.py:72
  10.4 0.1 multiply_add_fusion.1
  10.5 0.3 reduce-window.16
  10.8 0.2 slice_reduce_fusion
  11.0 0.2 reduce-window.19
  11.2 0.3 reduce-window.14
  11.5 0.2 slice_reduce_fusion.1
  11.7 0.2 reduce-window.15
  11.9 9.1 %gather_fusion.8 = s32[1024]{0:T(1024)S(1)} fusion(s32[4,1280]{1,0:T(4,128)S(1)} %get-tuple-element.42, s32[1024]{0:T(1024)S(1)} %bitcast.169), kind=kCustom, calls=%fused_computation.1.clone | custom fusion | bytes 16384 | tf_op jit(solution)/shard_map/jit(take_along_axis)/gather | solution.py:72
  21.0 0.1 fusion.46
  21.1 6.5 %gather_fusion.4 = s32[1024]{0:T(1024)S(1)} fusion(s32[1,1024]{1,0:T(1,128)S(1)} %copy-done.2, s32[1024]{0:T(1024)S(1)} %bitcast.163), kind=kCustom, calls=%fused_computation.6 | custom fusion | bytes 16384 | tf_op jit(solution)/shard_map/gather | solution.py:160
  27.7 6.5 %gather_fusion.5 = s32[1024]{0:T(1024)S(1)} fusion(s32[1,1024]{1,0:T(1,128)S(1)} %fusion.47, s32[1024]{0:T(1024)S(1)} %bitcast.164), kind=kCustom, calls=%fused_computation.7 | custom fusion | bytes 16384 | tf_op jit(solution)/shard_map/gather | solution.py:161
  34.2 6.5 %gather_fusion.2 = s32[1024]{0:T(1024)S(1)} fusion(s32[1,1024]{1,0:T(1,128)S(1)} %fusion.47, s32[1024]{0:T(1024)S(1)} %bitcast.161), kind=kCustom, calls=%fused_computation.4 | custom fusion | bytes 16384 | tf_op jit(solution)/shard_map/gather | solution.py:159
  41.0 12.5 %gather_fusion.6 = bf16[1024,8,128]{2,1,0:T(8,128)(2,1)} fusion(bf16[1,512,8,8,128]{4,2,3,1,0:T(8,128)(2,1)} %bitcast.178, s32[1024]{0:T(1024)S(1)} %bitcast.166), kind=kCustom, calls=%fused_computation.8 | custom fusion | bytes 4206592 | tf_op jit(solution)/shard_map/gather | solution.py:195
  53.5 4.5 %broadcast_select_fusion = bf16[1,4,256,8,128]{4,3,2,1,0:T(8,128)(2,1)} fusion(bf16[1,4,256,8,128]{4,3,2,1,0:T(8,128)(2,1)} %bitcast.174, pred[4,256]{1,0:T(4,128)(4,1)S(1)} %fusion.84), kind=kLoop, calls=%fused_computation.26 | loop fusion | flops 1048576 | bytes 4195328 | tf_op jit(solution)/shard_map/jit(_where)/select_n | solution.py:196
  58.0 0.5 collective-permute-start
  58.6 0.1 constant_dynamic-slice_fusion.1
  58.6 0.6 multiply_subtract_fusion
  59.3 2.5 %copy.91 = f32[8,8,32,256]{3,1,2,0:T(8,128)} copy(f32[8,8,32,256]{3,2,1,0:T(8,128)S(1)} %bitcast.176) | data formatting | bytes 4194304
  61.8 2.6 %copy.92 = f32[8,8,32,256]{3,1,2,0:T(8,128)} copy(f32[8,8,32,256]{3,2,1,0:T(8,128)S(1)} %bitcast.175) | data formatting | bytes 4194304
  64.4 2.4 %convolution_bitcast_fusion = f32[1,8192,4,128]{1,3,2,0:T(8,128)S(1)} fusion(bf16[1,8192,160]{1,2,0:T(8,128)(2,1)S(1)} %copy-done, bf16[1,160,512]{2,1,0:T(8,128)(2,1)S(1)} %copy-done.5), kind=kOutput, calls=%fused_computation.9 | convolution fusion | flops 1342177280 | bytes 19562496 | tf_op jit(solution)/shard_map/rtk,rkc->rtc/dot_general | solution.py:128
  66.7 5.9 %subtract_convert_fusion = (bf16[1,8192,4,64]{1,3,2,0:T(8,128)(2,1)}, bf16[1,8192,4,64]{1,3,2,0:T(8,128)(2,1)}) fusion(f32[1,8192,4,128]{1,3,2,0:T(8,128)S(1)} %convolution_bitcast_fusion, f32[8192,64]{0,1:T(8,128)} %bitcast.173, f32[8192,64]{0,1:T(8,128)} %bitcast.172), kind=kLoop, calls=%fused_computation.14 | loop fusion | flops 16777216 | bytes 29360128 | tf_op jit(solution)/shard_map/convert.3
  72.6 8.4 %copy.71 = bf16[1,8192,4,64]{3,1,2,0:T(8,128)(2,1)} copy(bf16[1,8192,4,64]{1,3,2,0:T(8,128)(2,1)} %get-tuple-element.22) | data formatting | bytes 8388608 | tf_op jit(solution)/shard_map/convert.2
  81.0 8.5 %copy.70 = bf16[1,8192,4,64]{3,1,2,0:T(8,128)(2,1)} copy(bf16[1,8192,4,64]{1,3,2,0:T(8,128)(2,1)} %get-tuple-element.21) | data formatting | bytes 8388608 | tf_op jit(solution)/shard_map/convert.3
  90.1 0.3 copy.68
  90.5 0.8 fusion.1
  91.3 22.4 %select_reduce_fusion.1 = (bf16[1024,4,128]{2,1,0:T(4,128)(2,1)S(1)}, bf16[1024,4,128]{2,1,0:T(4,128)(2,1)S(1)}, bf16[1,1024,8,4,128]{4,2,3,1,0:T(8,128)(2,1)}) fusion(pred[1024,8]{1,0:T(8,128)(4,1)S(1)} %copy.68, bf16[1,1024,8,4,64]{4,2,1,3,0:T(8,128)(2,1)} %bitcast.170, bf16[1,1024,8,4,64]{4,2,1,3,0:T(8,128)(2,1)} %bitcast.171), kind=kLoop, calls=%fused_computation.12 | loop fusion | flops 32505856 | bytes 18882560 | tf_op jit(solution)/shard_map/reduce_min | solution.py:139
  113.7 4.5 %select_convert_fusion = bf16[1024,4,128]{2,1,0:T(4,128)(2,1)} fusion(bf16[1024,4,128]{2,1,0:T(4,128)(2,1)S(1)} %get-tuple-element.7, bf16[1024,4,128]{2,1,0:T(4,128)(2,1)S(1)} %get-tuple-element.6, pred[1024]{0:T(1024)(128)(4,1)S(1)} %fusion.29), kind=kLoop, calls=%fused_computation.22 | loop fusion | flops 3145728 | bytes 3146752 | tf_op jit(solution)/shard_map/convert_element_type | solution.py:145
  118.3 7.6 %gather_fusion = bf16[1024,8,128]{2,1,0:T(8,128)(2,1)S(1)} fusion(bf16[1,1024,8,4,128]{4,2,3,1,0:T(8,128)(2,1)} %get-tuple-element.23, s32[1024]{0:T(1024)S(1)} %bitcast.165), kind=kCustom, calls=%fused_computation.2 | custom fusion | bytes 4206592 | tf_op jit(solution)/shard_map/gather | solution.py:164
  126.0 2.6 %fusion.40 = f32[4,256,8,8]{3,2,1,0:T(8,128)} fusion(bf16[4,256,8,128]{3,2,1,0:T(8,128)(2,1)S(1)} %bitcast.177, bf16[4096]{0:T(1024)(128)(2,1)S(1)} %reduce.21), kind=kOutput, calls=%fused_computation.83 | convolution fusion | flops 16777216 | bytes 2367488 | tf_op jit(solution)/shard_map/rhgd,rhcpd->rhgcp/dot_general | solution.py:166
  128.6 0.5 fusion.96
  129.1 2.8 %copy.75 = f32[4,256,8,8]{1,2,3,0:T(8,128)S(1)} copy(f32[4,256,8,8]{3,2,1,0:T(8,128)} %fusion.40) | data formatting | bytes 524288 | tf_op jit(solution)/shard_map/rhgd,rhcpd->rhgcp/dot_general | solution.py:166
  131.9 0.1 bitcast_reduce_fusion
  132.1 0.2 fusion.23
  132.2 0.2 fusion.20
  132.5 0.7 add.290
  133.2 6.8 %all-to-all-start.2 = ((f32[1,8,4]{2,0,1:T(1,128)}), f32[1,8,4]{2,0,1:T(1,128)S(1)}, u32[]{:S(2)}, u32[]{:S(2)}) async-start(f32[1,8,4]{2,0,1:T(1,128)} %bitcast.44), calls=%async_computation.2 | async-start | bytes 8192 | tf_op jit(solution)/shard_map/all_to_all | solution.py:223
  140.0 6.5 %gather_fusion.1 = s32[1024]{0:T(1024)S(1)} fusion(s32[1,1024]{1,0:T(1,128)S(1)} %copy-done.2, s32[1024]{0:T(1024)S(1)} %bitcast.162), kind=kCustom, calls=%fused_computation.3 | custom fusion | bytes 16384 | tf_op jit(solution)/shard_map/gather | solution.py:158
  146.5 0.7 max.55
  147.2 0.3 reshape.909
  147.5 0.2 fusion.95
  147.7 0.1 reshape.924
  147.8 0.2 fusion.31
  148.0 0.2 convolution_bitcast_fusion.1
  148.2 0.3 fusion.15
  148.5 2.1 copy.77
  150.6 12.5 %gather_fusion.3 = bf16[1024,8,128]{2,1,0:T(8,128)(2,1)} fusion(bf16[1,512,8,8,128]{4,2,3,1,0:T(8,128)(2,1)} %bitcast.179, s32[1024]{0:T(1024)S(1)} %bitcast.167), kind=kCustom, calls=%fused_computation.5 | custom fusion | bytes 4206592 | tf_op jit(solution)/shard_map/gather | solution.py:194
  163.1 6.0 %all-to-all-start.1 = ((f32[1,8,4]{2,0,1:T(1,128)}), f32[1,8,4]{2,0,1:T(1,128)S(1)}, u32[]{:S(2)}, u32[]{:S(2)}) async-start(f32[1,8,4]{2,0,1:T(1,128)} %bitcast.41), calls=%async_computation.1 | async-start | bytes 8192 | tf_op jit(solution)/shard_map/all_to_all | solution.py:220
  169.1 0.1 reshape.927
  169.2 0.1 copy.85
  169.3 6.3 %all-to-all-done.1 = f32[1,8,4]{2,0,1:T(1,128)S(1)} async-done(((f32[1,8,4]{2,0,1:T(1,128)}), f32[1,8,4]{2,0,1:T(1,128)S(1)}, u32[]{:S(2)}, u32[]{:S(2)}) %all-to-all-start.1) | async-done | bytes 160 | tf_op jit(solution)/shard_map/all_to_all | solution.py:220
  175.6 0.1 copy.80
  175.7 0.2 fusion.85
  175.9 5.5 %fusion.12 = f32[4,8,128]{2,1,0:T(8,128)} fusion(f32[4,8,128]{2,1,0:T(8,128)S(1)} %fusion.15, bf16[4,8,256,8]{3,1,2,0:T(8,128)(2,1)} %copy.77, bf16[1,4,256,8,128]{4,3,2,1,0:T(8,128)(2,1)} %bitcast.180, bf16[1,4,256,8,128]{4,3,2,1,0:T(8,128)(2,1)} %collective-permute-done, pred[4,256]{1,0:T(4,128)(4,1)S(1)} %reshape.1025), kind=kOutput, calls=%fused_computation.33 | convolution fusion | flops 17829888 | bytes 4359168 | tf_op jit(solution)/shard_map/rhgcp,rhcpd->rhgd/dot_general | solution.py:199
  181.4 3.3 %all-to-all-start = ((f32[1,32,128]{2,0,1:T(1,128)}), f32[1,32,128]{2,0,1:T(1,128)S(1)}, u32[]{:S(2)}, u32[]{:S(2)}) async-start(f32[1,32,128]{2,0,1:T(1,128)} %bitcast.39), calls=%async_computation | async-start | bytes 32768 | tf_op jit(solution)/shard_map/all_to_all | solution.py:226
  184.7 0.1 multiply_add_fusion.2
  184.8 0.1 copy.81
  184.9 6.3 %all-to-all-done = f32[1,32,128]{2,0,1:T(1,128)S(1)} async-done(((f32[1,32,128]{2,0,1:T(1,128)}), f32[1,32,128]{2,0,1:T(1,128)S(1)}, u32[]{:S(2)}, u32[]{:S(2)}) %all-to-all-start) | async-done | bytes 16416 | tf_op jit(solution)/shard_map/all_to_all | solution.py:226
  191.3 0.1 multiply_reduce_fusion
  191.3 0.1 fusion.88
  191.4 16.9 %all-gather = bf16[8,4,128]{2,1,0:T(4,128)(2,1)S(1)} all-gather(bf16[1,4,128]{2,1,0:T(4,128)(2,1)S(1)} %fusion.88), channel_id=1, replica_groups=mesh['grp'=2,'seq'=8,'pool'=2] {'seq'}, dimensions={0}, use_global_device_ids=true | all-gather | bytes 9216 | tf_op jit(solution)/shard_map/all_gather | solution.py:242
  208.3 0.6 reshape.928
  (78 shorter events, 1.0 us)
Async XLA Ops:
  0.0 64.4 %copy-start = (bf16[1,8192,160]{1,2,0:T(8,128)(2,1)S(1)}, bf16[1,8192,160]{1,2,0:T(8,128)(2,1)}, u32[]{:S(2)}) copy-start(bf16[1,8192,160]{1,2,0:T(8,128)(2,1)} %param.16) | copy-start | bytes 7864324
  1.2 9.3 %copy-start.2 = (s32[1,1024]{1,0:T(1,128)S(1)}, s32[1,1024]{1,0:T(1,128)}, u32[]{:S(2)}) copy-start(s32[1,1024]{1,0:T(1,128)} %param.24) | copy-start | bytes 12292
  53.5 5.1 %copy-start.11 = (f32[256,64]{0,1:T(8,128)S(1)}, f32[256,64]{0,1:T(8,128)}, u32[]{:S(2)}) copy-start(f32[256,64]{0,1:T(8,128)} %constant.31.clone) | copy-start | bytes 196612
  53.5 5.1 %copy-start.12 = (f32[256,64]{0,1:T(8,128)S(1)}, f32[256,64]{0,1:T(8,128)}, u32[]{:S(2)}) copy-start(f32[256,64]{0,1:T(8,128)} %constant.32.clone) | copy-start | bytes 196612
  53.5 5.2 %copy-start.6 = (f32[256,64]{0,1:T(8,128)S(1)}, f32[256,64]{0,1:T(8,128)}, u32[]{:S(2)}) copy-start(f32[256,64]{0,1:T(8,128)} %constant.86.clone) | copy-start | bytes 196612
  53.5 5.2 %copy-start.7 = (f32[256,64]{0,1:T(8,128)S(1)}, f32[256,64]{0,1:T(8,128)}, u32[]{:S(2)}) copy-start(f32[256,64]{0,1:T(8,128)} %constant.87.clone) | copy-start | bytes 196612
  58.0 117.9 %collective-permute-start = (bf16[1,4,256,8,128]{4,3,2,1,0:T(8,128)(2,1)}, bf16[1,4,256,8,128]{4,3,2,1,0:T(8,128)(2,1)}, u32[]{:S(2)}, u32[]{:S(2)}) collective-permute-start(bf16[1,4,256,8,128]{4,3,2,1,0:T(8,128)(2,1)} %broadcast_select_fusion), channel_id=1, source_target_pairs={{0,1},{1,0},{2,3},{3,2},{4,5},{5,4},{6,7},{7,6},{8,9},{9,8},{10,11... | collective-permute-start | bytes 6291464 | tf_op jit(solution)/shard_map/ppermute | solution.py:16
  61.8 2.6 %copy-start.5 = (bf16[1,160,512]{2,1,0:T(8,128)(2,1)S(1)}, bf16[1,160,512]{2,1,0:T(8,128)(2,1)}, u32[]{:S(2)}) copy-start(bf16[1,160,512]{2,1,0:T(8,128)(2,1)} %param.17) | copy-start | bytes 491524
  113.7 4.5 %copy-start.10 = (bf16[1,4096]{1,0:T(2,128)(2,1)S(1)}, bf16[1,4096]{1,0:T(2,128)(2,1)}, u32[]{:S(2)}) copy-start(bf16[1,4096]{1,0:T(2,128)(2,1)} %param.22) | copy-start | bytes 24580
  126.0 2.6 %copy-start.4 = (bf16[1024,4,128]{2,1,0:T(4,128)(2,1)S(1)}, bf16[1024,4,128]{2,1,0:T(4,128)(2,1)}, u32[]{:S(2)}) copy-start(bf16[1024,4,128]{2,1,0:T(4,128)(2,1)} %select_convert_fusion) | copy-start | bytes 3145732
  133.2 30.0 %all-to-all-start.2 = ((f32[1,8,4]{2,0,1:T(1,128)}), f32[1,8,4]{2,0,1:T(1,128)S(1)}, u32[]{:S(2)}, u32[]{:S(2)}) async-start(f32[1,8,4]{2,0,1:T(1,128)} %bitcast.44), calls=%async_computation.2 | async-start | bytes 8192 | tf_op jit(solution)/shard_map/all_to_all | solution.py:223
  140.0 7.2 %copy-start.3 = (bf16[1,1024,512]{2,1,0:T(8,128)(2,1)S(1)}, bf16[1,1024,512]{2,1,0:T(8,128)(2,1)}, u32[]{:S(2)}) copy-start(bf16[1,1024,512]{2,1,0:T(8,128)(2,1)} %param.19) | copy-start | bytes 3145732
  146.5 1.0 copy-start.8
  146.5 1.3 copy-start.9
  163.1 12.5 %all-to-all-start.1 = ((f32[1,8,4]{2,0,1:T(1,128)}), f32[1,8,4]{2,0,1:T(1,128)S(1)}, u32[]{:S(2)}, u32[]{:S(2)}) async-start(f32[1,8,4]{2,0,1:T(1,128)} %bitcast.41), calls=%async_computation.1 | async-start | bytes 8192 | tf_op jit(solution)/shard_map/all_to_all | solution.py:220
  175.9 33.0 %copy-start.1 = (bf16[1,8192,160]{1,2,0:T(8,128)(2,1)S(1)}, bf16[1,8192,160]{1,2,0:T(8,128)(2,1)}, u32[]{:S(2)}) copy-start(bf16[1,8192,160]{1,2,0:T(8,128)(2,1)} %param.16) | copy-start | bytes 7864324
  181.4 9.9 %all-to-all-start = ((f32[1,32,128]{2,0,1:T(1,128)}), f32[1,32,128]{2,0,1:T(1,128)S(1)}, u32[]{:S(2)}, u32[]{:S(2)}) async-start(f32[1,32,128]{2,0,1:T(1,128)} %bitcast.39), calls=%async_computation | async-start | bytes 32768 | tf_op jit(solution)/shard_map/all_to_all | solution.py:226
where the time goes:
time: 210 us; the launch traced here: 209 us
  local copies, waits for them, and re-layouts  107 us (51%)
  other arithmetic  42.6 us (20%)
  blocking collectives  16.9 us (8%)
  starting transfers between devices  16.7 us (8%)
  waiting for transfers between devices  12.7 us (6%)
  matrix products  11.7 us (6%)
    reduce_min x1, other arithmetic, local(): low_keys = jnp.min(jnp.where(token_mask, paged_keys, jnp.inf), axis=2)  22.4 us
    gather x4, local copies, waits for them, and re-layouts, slot_pages(): picked = jnp.take_along_axis(padded, offsets, axis=-1)  18.3 us
    another operation x11, local copies, waits for them, and re-layouts  17.5 us
    all_gather x1, blocking collectives, local(): all_rows = lax.all_gather(rows_out, 'seq', axis=0, tiled=True)  16.9 us
    gather x1, local copies, waits for them, and re-layouts, local(): local_rows = value_store[request_idx, my_rank, :, my_heads, :]  12.5 us
    gather x1, local copies, waits for them, and re-layouts, local(): outgoing_rows = value_store[request_idx, other_rank, :, other_heads, :]  12.5 us
    gather x1, local copies, waits for them, and re-layouts, local(): paged_keys[request_idx, my_local, :, local_heads[None, :, None], :]  7.64 us
    all_to_all x1, starting transfers between devices, local(): lax.all_to_all(weight_sum.reshape(1, row_total), 'seq', split_axis=1, con...  6.83 us
  transfers between devices with their start and end apart: 4, of which 2 were waited for; matrix products, arithmetic and copies ran while one was open for 47% of the time, Pallas kernels for 0%

commit v1 on v0

--- a/solution.py
+++ b/solution.py
@@ -10,6 +10,12 @@
 SEL = 1024
 CAPMIN = 64
 WIN = 64
+
+
+def trade_parts(x, mesh_axis, split, join):
+    shards = jnp.split(x, lax.axis_size(mesh_axis), axis=split)
+    received = lax.all_to_all(jnp.stack(shards), mesh_axis, 0, 0)
+    return jnp.concatenate(received, axis=join)
 
 
 def partner(x, axis, apart):
@@ -217,9 +223,7 @@
     row_total = requests * heads_here * group_size
     row_share = row_total // seq_count
     got_peak, got_sum, got_out = (
-        lax.all_to_all(
-            row_peak.reshape(1, row_total), "seq", split_axis=1, concat_axis=0, tiled=True
-        ),
+        trade_parts(row_peak.reshape(1, row_total), "seq", 1, 0),
         lax.all_to_all(
             weight_sum.reshape(1, row_total), "seq", split_axis=1, concat_axis=0, tiled=True
         ),

time: 210 us -> 216 us (1.029)
  local copies, waits for them, and re-layouts: 107 us -> 113 us
    all_to_all x1, waiting for transfers between devices: 6.31 us -> 0.01 us  [trade_parts(): received = lax.all_to_all(jnp.stack(shards), mesh_axis, 0, 0)]
    all_to_all x1, waiting for transfers between devices: 0.01 us -> 6.31 us  [local(): lax.all_to_all(weight_sum.reshape(1, row_total), 'seq', split_axis=1, con...]
    unnamed x35 -> x42, local copies, waits for them, and re-layouts: 5.17 us -> 9.37 us
    another operation x11 -> x12, local copies, waits for them, and re-layouts: 17.5 us -> 19.2 us
  transfers between devices with their start and end apart: 4 -> 4, of which waited for: 2 -> 2; matrix products, arithmetic and copies ran while one was open for 47% -> 48% of each run, Pallas kernels for 0% -> 0%
where the time goes in v1:
time: 216 us; the launch traced here: 215 us
  local copies, waits for them, and re-layouts  113 us (52%)
  other arithmetic  42.8 us (20%)
  blocking collectives  16.9 us (8%)
  starting transfers between devices  16.7 us (8%)
  waiting for transfers between devices  12.7 us (6%)
  matrix products  11.7 us (5%)
    reduce_min x1, other arithmetic, local(): low_keys = jnp.min(jnp.where(token_mask, paged_keys, jnp.inf), axis=2)  23.4 us
    another operation x11, local copies, waits for them, and re-layouts  18.6 us
    gather x4, local copies, waits for them, and re-layouts, slot_pages(): picked = jnp.take_along_axis(padded, offsets, axis=-1)  18.3 us
    all_gather x1, blocking collectives, local(): all_rows = lax.all_gather(rows_out, 'seq', axis=0, tiled=True)  16.9 us
    gather x1, local copies, waits for them, and re-layouts, local(): local_rows = value_store[request_idx, my_rank, :, my_heads, :]  12.5 us
    gather x1, local copies, waits for them, and re-layouts, local(): outgoing_rows = value_store[request_idx, other_rank, :, other_heads, :]  12.5 us
    unnamed x42, local copies, waits for them, and re-layouts  9.37 us
    gather x1, local copies, waits for them, and re-layouts, local(): paged_keys[request_idx, my_local, :, local_heads[None, :, None], :]  7.64 us
  transfers between devices with their start and end apart: 4, of which 2 were waited for; matrix products, arithmetic and copies ran while one was open for 48% of the time, Pallas kernels for 0%

profile of v1, /device:TPU:0, one launch (start us, length us, event | category | flops | bytes accessed | tf_op | source)
XLA Modules:
  0.0 214.7 jit_solution(8264000936126237734)
XLA Ops:
  0.0 1.1 convert_reduce_fusion.1
  1.1 0.1 fusion.74
  1.2 9.1 %gather_fusion.7 = s32[1024]{0:T(1024)S(1)} fusion(s32[4,1280]{1,0:T(4,128)S(1)} %get-tuple-element.43, s32[1024]{0:T(1024)S(1)} %bitcast.183), kind=kCustom, calls=%fused_computation.clone | custom fusion | bytes 16384 | tf_op jit(solution)/shard_map/jit(take_along_axis)/gather | solution.py:78
  10.5 0.3 reduce-window.16
  10.8 0.2 slice_reduce_fusion
  11.0 0.2 reduce-window.19
  11.2 0.3 reduce-window.14
  11.5 0.2 slice_reduce_fusion.1
  11.7 0.2 reduce-window.15
  11.9 9.1 %gather_fusion.8 = s32[1024]{0:T(1024)S(1)} fusion(s32[4,1280]{1,0:T(4,128)S(1)} %get-tuple-element.42, s32[1024]{0:T(1024)S(1)} %bitcast.184), kind=kCustom, calls=%fused_computation.1.clone | custom fusion | bytes 16384 | tf_op jit(solution)/shard_map/jit(take_along_axis)/gather | solution.py:78
  21.1 6.5 %gather_fusion.4 = s32[1024]{0:T(1024)S(1)} fusion(s32[1,1024]{1,0:T(1,128)S(1)} %copy-done.2, s32[1024]{0:T(1024)S(1)} %bitcast.178), kind=kCustom, calls=%fused_computation.6 | custom fusion | bytes 16384 | tf_op jit(solution)/shard_map/gather | solution.py:166
  27.7 6.5 %gather_fusion.5 = s32[1024]{0:T(1024)S(1)} fusion(s32[1,1024]{1,0:T(1,128)S(1)} %fusion.47, s32[1024]{0:T(1024)S(1)} %bitcast.179), kind=kCustom, calls=%fused_computation.7 | custom fusion | bytes 16384 | tf_op jit(solution)/shard_map/gather | solution.py:167
  34.2 6.5 %gather_fusion.2 = s32[1024]{0:T(1024)S(1)} fusion(s32[1,1024]{1,0:T(1,128)S(1)} %fusion.47, s32[1024]{0:T(1024)S(1)} %bitcast.176), kind=kCustom, calls=%fused_computation.4 | custom fusion | bytes 16384 | tf_op jit(solution)/shard_map/gather | solution.py:165
  41.0 12.5 %gather_fusion.6 = bf16[1024,8,128]{2,1,0:T(8,128)(2,1)} fusion(bf16[1,512,8,8,128]{4,2,3,1,0:T(8,128)(2,1)} %bitcast.193, s32[1024]{0:T(1024)S(1)} %bitcast.181), kind=kCustom, calls=%fused_computation.8 | custom fusion | bytes 4206592 | tf_op jit(solution)/shard_map/gather | solution.py:201
  53.5 4.5 %broadcast_select_fusion = bf16[1,4,256,8,128]{4,3,2,1,0:T(8,128)(2,1)} fusion(bf16[1,4,256,8,128]{4,3,2,1,0:T(8,128)(2,1)} %bitcast.189, pred[4,256]{1,0:T(4,128)(4,1)S(1)} %fusion.84), kind=kLoop, calls=%fused_computation.26 | loop fusion | flops 1048576 | bytes 4195328 | tf_op jit(solution)/shard_map/jit(_where)/select_n | solution.py:202
  58.0 0.5 collective-permute-start
  58.6 0.6 multiply_subtract_fusion
  59.3 2.5 %copy.88 = f32[8,8,32,256]{3,1,2,0:T(8,128)} copy(f32[8,8,32,256]{3,2,1,0:T(8,128)S(1)} %bitcast.191) | data formatting | bytes 4194304
  61.8 2.6 %copy.89 = f32[8,8,32,256]{3,1,2,0:T(8,128)} copy(f32[8,8,32,256]{3,2,1,0:T(8,128)S(1)} %bitcast.190) | data formatting | bytes 4194304
  64.4 2.4 %convolution_bitcast_fusion = f32[1,8192,4,128]{1,3,2,0:T(8,128)S(1)} fusion(bf16[1,8192,160]{1,2,0:T(8,128)(2,1)S(1)} %copy-done, bf16[1,160,512]{2,1,0:T(8,128)(2,1)S(1)} %copy-done.5), kind=kOutput, calls=%fused_computation.9 | convolution fusion | flops 1342177280 | bytes 19562496 | tf_op jit(solution)/shard_map/rtk,rkc->rtc/dot_general | solution.py:134
  66.7 5.9 %subtract_convert_fusion = (bf16[1,8192,4,64]{1,3,2,0:T(8,128)(2,1)}, bf16[1,8192,4,64]{1,3,2,0:T(8,128)(2,1)}) fusion(f32[1,8192,4,128]{1,3,2,0:T(8,128)S(1)} %convolution_bitcast_fusion, f32[8192,64]{0,1:T(8,128)} %bitcast.188, f32[8192,64]{0,1:T(8,128)} %bitcast.187), kind=kLoop, calls=%fused_computation.14 | loop fusion | flops 16777216 | bytes 29360128 | tf_op jit(solution)/shard_map/convert.3
  72.6 8.4 %copy.69 = bf16[1,8192,4,64]{3,1,2,0:T(8,128)(2,1)} copy(bf16[1,8192,4,64]{1,3,2,0:T(8,128)(2,1)} %get-tuple-element.22) | data formatting | bytes 8388608 | tf_op jit(solution)/shard_map/convert.2
  81.0 8.5 %copy.68 = bf16[1,8192,4,64]{3,1,2,0:T(8,128)(2,1)} copy(bf16[1,8192,4,64]{1,3,2,0:T(8,128)(2,1)} %get-tuple-element.21) | data formatting | bytes 8388608 | tf_op jit(solution)/shard_map/convert.3
  90.1 0.3 copy.66
  90.5 23.4 %select_reduce_fusion.1 = (bf16[1024,4,128]{2,1,0:T(4,128)(2,1)}, bf16[1024,4,128]{2,1,0:T(4,128)(2,1)}, bf16[1,1024,8,4,128]{4,2,3,1,0:T(8,128)(2,1)}) fusion(pred[1024,8]{1,0:T(8,128)(4,1)S(1)} %copy.66, bf16[1,1024,8,4,64]{4,2,1,3,0:T(8,128)(2,1)} %bitcast.185, bf16[1,1024,8,4,64]{4,2,1,3,0:T(8,128)(2,1)} %bitcast.186), kind=kLoop, calls=%fused_computation.12 | loop fusion | flops 32505856 | bytes 18882560 | tf_op jit(solution)/shard_map/reduce_min | solution.py:145
  114.0 7.6 %gather_fusion = bf16[1024,8,128]{2,1,0:T(8,128)(2,1)S(1)} fusion(bf16[1,1024,8,4,128]{4,2,3,1,0:T(8,128)(2,1)} %get-tuple-element.23, s32[1024]{0:T(1024)S(1)} %bitcast.180), kind=kCustom, calls=%fused_computation.2 | custom fusion | bytes 4206592 | tf_op jit(solution)/shard_map/gather | solution.py:170
  121.6 2.6 %fusion.40 = f32[4,256,8,8]{3,2,1,0:T(8,128)} fusion(bf16[4,256,8,128]{3,2,1,0:T(8,128)(2,1)S(1)} %bitcast.192, bf16[4096]{0:T(1024)(128)(2,1)S(1)} %reduce.21), kind=kOutput, calls=%fused_computation.91 | convolution fusion | flops 16777216 | bytes 2367488 | tf_op jit(solution)/shard_map/rhgd,rhcpd->rhgcp/dot_general | solution.py:172
  124.2 3.0 %copy.73 = f32[4,256,8,8]{1,2,3,0:T(8,128)S(1)} copy(f32[4,256,8,8]{3,2,1,0:T(8,128)} %fusion.40) | data formatting | bytes 524288 | tf_op jit(solution)/shard_map/rhgd,rhcpd->rhgcp/dot_general | solution.py:172
  127.2 0.8 fusion.1
  128.0 3.8 %select_convert_fusion = bf16[1024,4,128]{2,1,0:T(4,128)(2,1)S(1)} fusion(bf16[1024,4,128]{2,1,0:T(4,128)(2,1)S(1)} %copy-done.4, bf16[1024,4,128]{2,1,0:T(4,128)(2,1)S(1)} %copy-done.3, pred[1024]{0:T(1024)(128)(4,1)S(1)} %fusion.29), kind=kLoop, calls=%fused_computation.22 | loop fusion | flops 3145728 | bytes 3146752 | tf_op jit(solution)/shard_map/convert_element_type | solution.py:151
  131.8 0.5 fusion.96
  132.3 0.1 bitcast_reduce_fusion
  132.5 0.1 max.53
  132.6 0.5 constant_dynamic-update-slice_fusion.7
  133.1 0.6 constant_dynamic-update-slice_fusion.6
  133.7 0.6 constant_dynamic-update-slice_fusion.5
  134.4 0.6 constant_dynamic-update-slice_fusion.4
  135.0 0.7 constant_dynamic-update-slice_fusion.3
  135.6 0.6 constant_dynamic-update-slice_fusion.2
  136.2 0.6 constant_dynamic-update-slice_fusion.1
  136.8 0.6 constant_dynamic-update-slice_fusion
  137.4 6.8 %all-to-all-start.1 = ((f32[8,1,4]{2,1,0:T(1,128)}), f32[8,1,4]{2,1,0:T(1,128)S(1)}, u32[]{:S(2)}, u32[]{:S(2)}) async-start(f32[8,1,4]{2,1,0:T(1,128)} %constant_dynamic-update-slice_fusion), calls=%async_computation.1 | async-start | bytes 8192 | tf_op jit(solution)/shard_map/all_to_all | solution.py:17
  144.2 6.4 %gather_fusion.1 = s32[1024]{0:T(1024)S(1)} fusion(s32[1,1024]{1,0:T(1,128)S(1)} %copy-done.2, s32[1024]{0:T(1024)S(1)} %bitcast.177), kind=kCustom, calls=%fused_computation.3 | custom fusion | bytes 16384 | tf_op jit(solution)/shard_map/gather | solution.py:164
  150.7 0.2 fusion.20
  150.9 2.1 copy.75
  153.0 1.3 reshape.903
  154.4 12.5 %gather_fusion.3 = bf16[1024,8,128]{2,1,0:T(8,128)(2,1)} fusion(bf16[1,512,8,8,128]{4,2,3,1,0:T(8,128)(2,1)} %bitcast.194, s32[1024]{0:T(1024)S(1)} %bitcast.182), kind=kCustom, calls=%fused_computation.5 | custom fusion | bytes 4206592 | tf_op jit(solution)/shard_map/gather | solution.py:200
  167.0 0.2 fusion.95
  167.2 0.1 reshape.919
  167.4 0.2 fusion.31
  167.5 0.2 convolution_bitcast_fusion.1
  167.7 0.2 fusion.23
  167.9 0.3 fusion.15
  168.2 0.7 add.290
  169.0 6.0 %all-to-all-start.2 = ((f32[1,8,4]{2,0,1:T(1,128)}), f32[1,8,4]{2,0,1:T(1,128)S(1)}, u32[]{:S(2)}, u32[]{:S(2)}) async-start(f32[1,8,4]{2,0,1:T(1,128)} %bitcast.51), calls=%async_computation.2 | async-start | bytes 8192 | tf_op jit(solution)/shard_map/all_to_all | solution.py:227
  175.1 6.3 %all-to-all-done.2 = f32[1,8,4]{2,0,1:T(1,128)S(1)} async-done(((f32[1,8,4]{2,0,1:T(1,128)}), f32[1,8,4]{2,0,1:T(1,128)S(1)}, u32[]{:S(2)}, u32[]{:S(2)}) %all-to-all-start.2) | async-done | bytes 160 | tf_op jit(solution)/shard_map/all_to_all | solution.py:227
  181.5 0.2 fusion.85
  181.7 5.5 %fusion.12 = f32[4,8,128]{2,1,0:T(8,128)} fusion(f32[4,8,128]{2,1,0:T(8,128)S(1)} %fusion.15, bf16[4,8,256,8]{3,1,2,0:T(8,128)(2,1)} %copy.75, bf16[1,4,256,8,128]{4,3,2,1,0:T(8,128)(2,1)} %bitcast.195, bf16[1,4,256,8,128]{4,3,2,1,0:T(8,128)(2,1)} %collective-permute-done, pred[4,256]{1,0:T(4,128)(4,1)S(1)} %reshape.1020), kind=kOutput, calls=%fused_computation.33 | convolution fusion | flops 17829888 | bytes 4359168 | tf_op jit(solution)/shard_map/rhgcp,rhcpd->rhgd/dot_general | solution.py:205
  187.2 3.3 %all-to-all-start = ((f32[1,32,128]{2,0,1:T(1,128)}), f32[1,32,128]{2,0,1:T(1,128)S(1)}, u32[]{:S(2)}, u32[]{:S(2)}) async-start(f32[1,32,128]{2,0,1:T(1,128)} %bitcast.39), calls=%async_computation | async-start | bytes 32768 | tf_op jit(solution)/shard_map/all_to_all | solution.py:230
  190.5 0.1 multiply_add_fusion.2
  190.7 6.3 %all-to-all-done = f32[1,32,128]{2,0,1:T(1,128)S(1)} async-done(((f32[1,32,128]{2,0,1:T(1,128)}), f32[1,32,128]{2,0,1:T(1,128)S(1)}, u32[]{:S(2)}, u32[]{:S(2)}) %all-to-all-start) | async-done | bytes 16416 | tf_op jit(solution)/shard_map/all_to_all | solution.py:230
  197.0 0.1 multiply_reduce_fusion
  197.2 16.9 %all-gather = bf16[8,4,128]{2,1,0:T(4,128)(2,1)S(1)} all-gather(bf16[1,4,128]{2,1,0:T(4,128)(2,1)S(1)} %fusion.88), channel_id=1, replica_groups=mesh['grp'=2,'seq'=8,'pool'=2] {'seq'}, dimensions={0}, use_global_device_ids=true | all-gather | bytes 9216 | tf_op jit(solution)/shard_map/all_gather | solution.py:246
  214.1 0.6 reshape.923
  (86 shorter events, 1.6 us)
Async XLA Ops:
  0.0 64.4 %copy-start = (bf16[1,8192,160]{1,2,0:T(8,128)(2,1)S(1)}, bf16[1,8192,160]{1,2,0:T(8,128)(2,1)}, u32[]{:S(2)}) copy-start(bf16[1,8192,160]{1,2,0:T(8,128)(2,1)} %param.16) | copy-start | bytes 7864324
  1.2 9.3 %copy-start.2 = (s32[1,1024]{1,0:T(1,128)S(1)}, s32[1,1024]{1,0:T(1,128)}, u32[]{:S(2)}) copy-start(s32[1,1024]{1,0:T(1,128)} %param.24) | copy-start | bytes 12292
  53.5 5.1 %copy-start.11 = (f32[256,64]{0,1:T(8,128)S(1)}, f32[256,64]{0,1:T(8,128)}, u32[]{:S(2)}) copy-start(f32[256,64]{0,1:T(8,128)} %constant.31.clone) | copy-start | bytes 196612
  53.5 5.1 %copy-start.12 = (f32[256,64]{0,1:T(8,128)S(1)}, f32[256,64]{0,1:T(8,128)}, u32[]{:S(2)}) copy-start(f32[256,64]{0,1:T(8,128)} %constant.32.clone) | copy-start | bytes 196612
  53.5 5.2 %copy-start.6 = (f32[256,64]{0,1:T(8,128)S(1)}, f32[256,64]{0,1:T(8,128)}, u32[]{:S(2)}) copy-start(f32[256,64]{0,1:T(8,128)} %constant.86.clone) | copy-start | bytes 196612
  53.5 5.2 %copy-start.7 = (f32[256,64]{0,1:T(8,128)S(1)}, f32[256,64]{0,1:T(8,128)}, u32[]{:S(2)}) copy-start(f32[256,64]{0,1:T(8,128)} %constant.87.clone) | copy-start | bytes 196612
  58.0 123.7 %collective-permute-start = (bf16[1,4,256,8,128]{4,3,2,1,0:T(8,128)(2,1)}, bf16[1,4,256,8,128]{4,3,2,1,0:T(8,128)(2,1)}, u32[]{:S(2)}, u32[]{:S(2)}) collective-permute-start(bf16[1,4,256,8,128]{4,3,2,1,0:T(8,128)(2,1)} %broadcast_select_fusion), channel_id=1, source_target_pairs={{0,1},{1,0},{2,3},{3,2},{4,5},{5,4},{6,7},{7,6},{8,9},{9,8},{10,11... | collective-permute-start | bytes 6291464 | tf_op jit(solution)/shard_map/ppermute | solution.py:22
  61.8 2.6 %copy-start.5 = (bf16[1,160,512]{2,1,0:T(8,128)(2,1)S(1)}, bf16[1,160,512]{2,1,0:T(8,128)(2,1)}, u32[]{:S(2)}) copy-start(bf16[1,160,512]{2,1,0:T(8,128)(2,1)} %param.17) | copy-start | bytes 491524
  81.0 9.5 %copy-start.10 = (bf16[1,4096]{1,0:T(2,128)(2,1)S(1)}, bf16[1,4096]{1,0:T(2,128)(2,1)}, u32[]{:S(2)}) copy-start(bf16[1,4096]{1,0:T(2,128)(2,1)} %param.22) | copy-start | bytes 24580
  124.2 3.8 %copy-start.3 = (bf16[1024,4,128]{2,1,0:T(4,128)(2,1)S(1)}, bf16[1024,4,128]{2,1,0:T(4,128)(2,1)}, u32[]{:S(2)}) copy-start(bf16[1024,4,128]{2,1,0:T(4,128)(2,1)} %get-tuple-element.6) | copy-start | bytes 3145732
  124.2 3.8 %copy-start.4 = (bf16[1024,4,128]{2,1,0:T(4,128)(2,1)S(1)}, bf16[1024,4,128]{2,1,0:T(4,128)(2,1)}, u32[]{:S(2)}) copy-start(bf16[1024,4,128]{2,1,0:T(4,128)(2,1)} %get-tuple-element.7) | copy-start | bytes 3145732
  137.4 31.6 %all-to-all-start.1 = ((f32[8,1,4]{2,1,0:T(1,128)}), f32[8,1,4]{2,1,0:T(1,128)S(1)}, u32[]{:S(2)}, u32[]{:S(2)}) async-start(f32[8,1,4]{2,1,0:T(1,128)} %constant_dynamic-update-slice_fusion), calls=%async_computation.1 | async-start | bytes 8192 | tf_op jit(solution)/shard_map/all_to_all | solution.py:17
  154.4 12.6 %copy-start.8 = (bf16[1,64,512]{2,1,0:T(8,128)(2,1)S(1)}, bf16[1,64,512]{2,1,0:T(8,128)(2,1)}, u32[]{:S(2)}) copy-start(bf16[1,64,512]{2,1,0:T(8,128)(2,1)} %param.20) | copy-start | bytes 196612
  154.4 12.9 %copy-start.9 = (bf16[1,64,512]{2,1,0:T(8,128)(2,1)S(1)}, bf16[1,64,512]{2,1,0:T(8,128)(2,1)}, u32[]{:S(2)}) copy-start(bf16[1,64,512]{2,1,0:T(8,128)(2,1)} %param.21) | copy-start | bytes 196612
  169.0 12.4 %all-to-all-start.2 = ((f32[1,8,4]{2,0,1:T(1,128)}), f32[1,8,4]{2,0,1:T(1,128)S(1)}, u32[]{:S(2)}, u32[]{:S(2)}) async-start(f32[1,8,4]{2,0,1:T(1,128)} %bitcast.51), calls=%async_computation.2 | async-start | bytes 8192 | tf_op jit(solution)/shard_map/all_to_all | solution.py:227
  181.7 33.0 %copy-start.1 = (bf16[1,8192,160]{1,2,0:T(8,128)(2,1)S(1)}, bf16[1,8192,160]{1,2,0:T(8,128)(2,1)}, u32[]{:S(2)}) copy-start(bf16[1,8192,160]{1,2,0:T(8,128)(2,1)} %param.16) | copy-start | bytes 7864324
  187.2 9.9 %all-to-all-start = ((f32[1,32,128]{2,0,1:T(1,128)}), f32[1,32,128]{2,0,1:T(1,128)S(1)}, u32[]{:S(2)}, u32[]{:S(2)}) async-start(f32[1,32,128]{2,0,1:T(1,128)} %bitcast.39), calls=%async_computation | async-start | bytes 32768 | tf_op jit(solution)/shard_map/all_to_all | solution.py:230
